TPU v7x, 512 devices: a whole 4x8x8 slice. The times are simulated.
512 devices in a mesh: ka: 8 (over y_hi, core), pb: 16 (over y_lo, z), row: 4 (over x).
Axes of the slice: x: 4, y: 8 (y_hi: 4, y_lo: 2; y = y_hi * 2 + y_lo), z: 8, core: 2. Of those that a mesh axis runs over, the one named last changes fastest.
Arguments:
- coupling: bfloat16 [64, 64, 20736], P('pb', ('ka', 'row')), may hold values from -1 to 1
- rotation: bfloat16 [64, 36, 36], P('pb'), may hold values from -1 to 1
- freq: float32 [64, 36], P('pb'), may hold values from 0.02 to 0.3
- eigvec: bfloat16 [1024, 24, 24], P(('ka', 'row')), may hold values from -1.25 to 1.25
- energies: float32 [1024, 24], P(('ka', 'row')), may hold values from -1.5 to 1.5
- window: int32 [1024], P(('ka', 'row')), may hold values from 12 to 24
- kq_index: int32 [64, 1024], P('pb'), may hold values from 0 to 1023, as said below
- kpoints: float32 [1024, 3], replicated, may hold values from 0 to 1
- lattice: int32 [64, 3], replicated, may hold values from -3 to 3
Outputs:
- electron: float32 [1024, 24], P(('ka', 'row'))
- phonon: float32 [64, 36], P('pb')
Inputs may be any that keep to these rules, and one draw needn't show every extreme that they name: The k-points form a shifted grid of 1024 points, (1024 // 64) x 8 x 8, listed in an order drawn from the seed; each q-point is a vector of that grid without the shift. kq_index[q, k] is the index of the k-point equal to kpoints[k] plus the q-point's vector modulo 1, so each row of kq_index is a permutation of 0 to 1023.
All inputs are finite; a program needn't handle non-finite values.
Results may differ from a plain program's by a relative error of at most 0.00089.
Values may be sent and summed in bfloat16 or wider, within the bound.
A program may use at most 128 MiB of HBM per device.

v0:
```python
import math
import jax
import jax.numpy as jnp
from jax import lax
from jax.sharding import PartitionSpec as P

SIGMA = 0.1
THERMAL_ENERGY_KT = 0.2


def phase_table(lattice, kpoint_rows):
    rvec = lattice.astype(jnp.float32)
    argument = (
        rvec[:, 0:1] * kpoint_rows[:, 0][None, :]
        + rvec[:, 1:2] * kpoint_rows[:, 1][None, :]
        + rvec[:, 2:3] * kpoint_rows[:, 2][None, :]
    )
    return jnp.cos(2.0 * math.pi * argument).astype(jnp.bfloat16)


def block_terms(
    coup_rows, phase_cols, rot_rows, freq_rows, eig_k, eig_kq, level_k, level_kq, lim_k, lim_kq
):
    q_block = coup_rows.shape[0]
    k_block = phase_cols.shape[1]
    columns = q_block * k_block
    n_modes = rot_rows.shape[1]
    n_bands = eig_k.shape[0]
    norm = 1.0 / (math.sqrt(2.0 * math.pi) * SIGMA)
    bloch = jnp.einsum(
        "qrf,rk->fqk", coup_rows, phase_cols, preferred_element_type=jnp.float32
    ).astype(jnp.bfloat16)
    bloch = bloch.reshape(n_modes, n_bands, n_bands, columns)
    rot_cols = jnp.repeat(jnp.transpose(rot_rows, (1, 2, 0)), k_block, axis=2)
    modal = jnp.einsum(
        "amnc,abc->bmnc", bloch, rot_cols, preferred_element_type=jnp.float32
    ).astype(jnp.bfloat16)
    eig_k_cols = jnp.tile(eig_k, (1, 1, q_block))
    right = jnp.einsum(
        "bmjc,jnc->bmnc", modal, eig_k_cols, preferred_element_type=jnp.float32
    ).astype(jnp.bfloat16)
    coupled = jnp.einsum("imc,binc->bmnc", eig_kq, right, preferred_element_type=jnp.float32)
    level_k_cols = jnp.tile(level_k, (1, q_block))
    lim_k_cols = jnp.tile(lim_k, (q_block,))
    freq_cols = jnp.repeat(freq_rows.T, k_block, axis=1)
    diff = level_kq[None, :, None, :] - level_k_cols[None, None, :, :] - freq_cols[:, None, None, :]
    delta = jnp.exp(-(diff * diff) / (2.0 * SIGMA * SIGMA)) * norm
    bands = jnp.arange(n_bands).astype(jnp.float32)
    mask_m = (bands[:, None] < lim_kq[None, :]).astype(jnp.float32)
    mask_n = (bands[:, None] < lim_k_cols[None, :]).astype(jnp.float32)
    strength = coupled * coupled * delta * mask_m[None, :, None, :] * mask_n[None, None, :, :]
    filling_initial = jax.nn.sigmoid(-level_k_cols / THERMAL_ENERGY_KT)
    filling_final = jax.nn.sigmoid(-level_kq / THERMAL_ENERGY_KT)
    elec = jnp.sum(strength, axis=(0, 1)).reshape(n_bands, q_block, k_block).sum(axis=1)
    phon = jnp.sum(
        strength * (filling_initial[None, None, :, :] - filling_final[None, :, None, :]),
        axis=(1, 2),
    )
    phon = phon.reshape(n_modes, q_block, k_block).sum(axis=2)
    return (elec, phon)


def on_device(coupling, rotation, freq, eigvec, energies, window, kq_index, kpoints, lattice):
    n_ka = lax.axis_size("ka")
    n_row = lax.axis_size("row")
    n_pb = lax.axis_size("pb")
    k_dev = eigvec.shape[0]
    q_dev = rotation.shape[0]
    n_bands = eigvec.shape[1]
    n_modes = rotation.shape[1]
    total_k = k_dev * n_ka * n_row
    total_q = q_dev * n_pb
    eigen_grid = lax.all_gather(eigvec, ("ka", "row"), axis=0, tiled=True)
    level_all, limit_all = (
        lax.all_gather(energies, ("ka", "row"), axis=0, tiled=True),
        lax.all_gather(window.astype(jnp.float32), ("ka", "row"), axis=0, tiled=True),
    )
    eig_cols = jnp.transpose(eigen_grid, (1, 2, 0))
    level_cols = level_all.T
    ka_pos = lax.axis_index("ka")
    row_pos = lax.axis_index("row")
    coup_full = lax.all_gather(coupling, ("ka", "row"), axis=1, tiled=True)
    q_start = jnp.int32(0)
    k_start = (ka_pos * n_row + row_pos) * k_dev
    kq_mine = lax.dynamic_slice(kq_index, (q_start, k_start), (q_dev, k_dev))
    kp_mine = lax.dynamic_slice(kpoints, (k_start, jnp.int32(0)), (k_dev, 3))
    eig_mine = lax.dynamic_slice_in_dim(eig_cols, k_start, k_dev, 2)
    lev_mine = lax.dynamic_slice_in_dim(level_cols, k_start, k_dev, 1)
    lim_mine = lax.dynamic_slice_in_dim(limit_all, k_start, k_dev, 0)
    phase_all = phase_table(lattice, kp_mine)
    k_block = min(k_dev, 128)
    elec_cols = [None] * (k_dev // k_block)
    index = kq_mine.reshape(-1)
    eig_kq = jnp.take(eig_cols, index, axis=2)
    level_kq = jnp.take(level_cols, index, axis=1)
    lim_kq = jnp.take(limit_all, index, axis=0)
    elec, phon = block_terms(
        coup_full, phase_all, rotation, freq, eig_mine, eig_kq, lev_mine, level_kq, lim_mine, lim_kq
    )
    elec_cols[0] = elec
    elec_local = elec_cols[0].T * (1.0 / (total_q * n_modes * n_bands))
    phon_local = phon.T * (1.0 / (total_k * n_bands))
    phonon = lax.psum(phon_local, ("ka", "row"))
    electron = lax.psum(elec_local, "pb")
    return (electron, phonon)


def solution(mesh):
    return jax.shard_map(
        on_device,
        mesh=mesh,
        in_specs=(
            P("pb", ("ka", "row"), None),
            P("pb", None, None),
            P("pb", None),
            P(("ka", "row"), None, None),
            P(("ka", "row"), None),
            P(("ka", "row")),
            P("pb", None),
            P(),
            P(),
        ),
        out_specs=(P(("ka", "row"), None), P("pb", None)),
        check_vma=False,
    )
```

profile of v0, /device:TPU:40, one launch (start us, length us, event | category | flops | bytes accessed | tf_op | source)
XLA Modules:
  0.0 554.0 jit_solution(66930285304489676)
XLA Ops:
  7.2 1.7 copy.47
  9.0 1.8 copy.49
  11.2 0.7 convert_element_type.50
  11.8 1.3 dynamic-slice.8
  13.8 0.8 convert_dynamic-update-slice_fusion
  14.5 78.9 %all-reduce = f32[1024]{0:T(1024)S(1)} all-reduce(f32[1024]{0:T(1024)S(1)} %convert_dynamic-update-slice_fusion), channel_id=1, replica_groups=mesh['ka'=8,'pb'=16,'row'=4] {'ka','row'}, use_global_device_ids=true, to_apply=%add | all-reduce | flops 1024 | bytes 8192
  93.6 1.0 gather_fusion.2
  94.6 0.8 copy.79
  95.5 0.1 copy.62
  95.7 82.7 %all-gather = f32[32,32,24]{1,2,0:T(8,128)S(1)} all-gather(f32[1,32,24]{1,2,0:T(8,128)} %bitcast.93), channel_id=1, replica_groups=mesh['ka'=8,'pb'=16,'row'=4] {'ka','row'}, dimensions={0}, use_global_device_ids=true | all-gather | bytes 101376 | tf_op jit(solution)/shard_map/all_gather | solution.py:75
  178.4 0.2 copy.57
  178.8 0.1 copy.61
  178.9 0.1 copy.64
  179.0 0.7 gather_fusion.1
  179.8 0.1 copy.65
  179.9 0.1 copy.59
  180.0 0.8 constant_dynamic-slice_fusion.1
  180.8 2.2 broadcast_subtract_fusion
  182.9 0.9 dynamic-slice_bitcast_fusion
  183.9 0.1 copy.48
  184.0 3.5 gather_fusion
  187.6 8.0 %fusion.4 = bf16[20736,4,32]{0,2,1:T(8,128)(2,1)} fusion(bf16[4,64,20736]{2,0,1:T(4,128)(2,1)} %all-gather.6.cloned.1.call-done, f32[32]{0:T(128)S(1)} %get-tuple-element.18, f32[64]{0:T(128)S(1)} %get-tuple-element.15, f32[32]{0:T(128)S(1)} %get-tuple-element.19, f32[64]{0:T(128)S(1)} %get-tuple-element.16, f32[32]{0:T(128)S(1)} %get-tuple-element.17, ...), kind=kOutput, calls=%fused_computation.10 | convolution fusion | flops 342407168 | bytes 15926400 | tf_op jit(solution)/shard_map/qrf,rk->fqk/dot_general | solution.py:30
  195.6 47.2 %reshape.253 = bf16[36,24,24,128]{2,1,0,3:T(8,128)(2,1)} reshape(bf16[20736,4,32]{0,2,1:T(8,128)(2,1)} %fusion.4) | data formatting | bytes 10616832 | tf_op jit(solution)/shard_map/reshape | solution.py:33
  242.8 0.1 tile.10
  242.9 0.2 broadcast_in_dim.40.clone
  243.1 23.0 %convert_bitcast_fusion = bf16[36,24,24,128]{0,2,1,3:T(8,128)(2,1)} fusion(bf16[24,24,128,1]{0,1,3,2:T(8,128)(2,1)S(1)} %bitcast.86, bf16[36,36,128,1]{1,0,3,2:T(8,128)(2,1)S(1)} %bitcast.85, bf16[36,24,24,128]{2,1,0,3:T(8,128)(2,1)} %reshape.253), kind=kOutput, calls=%fused_computation.15 | convolution fusion | flops 323813376 | bytes 11096064 | tf_op jit(solution)/shard_map/bmjc,jnc->bmnc/dot_general | solution.py:39
  266.1 69.3 %multiply_reduce_fusion = (f32[36,128]{0,1:T(8,128)S(1)}, f32[24,128]{0,1:T(8,128)S(1)}) fusion(f32[24,24,128]{0,1,2:T(8,128)} %get-tuple-element.22, f32[24,128]{0,1:T(8,128)S(1)} %copy.63, f32[24,128]{0,1:T(8,128)S(1)} %copy.62, f32[36,128]{0,1:T(8,128)S(1)} %bitcast.90, f32[24,24,128]{0,1,2:T(8,128)} %get-tuple-element.23, ...), kind=kOutput, calls=%fused_computation.6 | convolution fusion | flops 159318528 | bytes 6119552 | tf_op jit(solution)/shard_map/imc,binc->bmnc/dot_general | solution.py:42
  335.5 69.8 %psum.14 = f32[32,24]{1,0:T(8,128)S(1)} all-reduce(f32[32,24]{1,0:T(8,128)S(1)} %multiply_bitcast_fusion.1), channel_id=1, replica_groups=mesh['ka'=8,'pb'=16,'row'=4] {'pb'}, use_global_device_ids=true, to_apply=%region_2.3 | all-reduce | flops 768 | bytes 6144 | tf_op jit(solution)/shard_map/psum | solution.py:104
  405.3 0.7 copy.67
  405.9 0.1 copy.78
  406.0 140.5 %psum.15 = f32[4,36]{0,1:T(8,128)S(1)} all-reduce(f32[4,36]{0,1:T(8,128)S(1)} %multiply_bitcast_fusion), channel_id=1, replica_groups=mesh['ka'=8,'pb'=16,'row'=4] {'ka','row'}, use_global_device_ids=true, to_apply=%region_5.6 | all-reduce | flops 144 | bytes 1152 | tf_op jit(solution)/shard_map/psum | solution.py:103
  546.5 0.7 copy.68
  (39 shorter events, 1.1 us)
Async XLA Ops:
  7.2 3.7 copy-start
  7.2 175.7 %all-gather.4.cloned.1.call-start = ((), (), s32[]{:S(2)}) async-start(), calls=%async_computation | async-start | bytes 6488064 | tf_op jit(solution)/shard_map/all_gather | solution.py:73
  9.0 178.6 %all-gather.6.cloned.1.call-start = ((), (), s32[]{:S(2)}) async-start(), calls=%async_computation.1 | async-start | bytes 10948608 | tf_op jit(solution)/shard_map/all_gather | solution.py:82
  243.1 23.0 %copy-start.2 = (f32[4,36]{1,0:T(4,128)S(1)}, f32[4,36]{1,0:T(4,128)}, u32[]{:S(2)}) copy-start(f32[4,36]{1,0:T(4,128)} %param.11) | copy-start | bytes 1732
  266.1 281.1 %copy-start.1 = (s32[4,1024]{1,0:T(4,128)S(1)}, s32[4,1024]{1,0:T(4,128)}, u32[]{:S(2)}) copy-start(s32[4,1024]{1,0:T(4,128)} %param.15) | copy-start | bytes 49156
Sparse Core Ops, SparseCore 0:
  11.1 75.5 all-gather.3
  89.9 93.6 all-gather.5
where the time goes:
time: 555 us; the launch traced here: 554 us
  blocking collectives  372 us (67%)
  matrix products  100 us (18%)
  local copies, waits for them, and re-layouts  63 us (11%)
  between operations  14.9 us (3%)
    psum x1, blocking collectives, on_device(): phonon = lax.psum(phon_local, ('ka', 'row'))  140 us
    all_gather x1, blocking collectives, on_device(): lax.all_gather(energies, ('ka', 'row'), axis=0, tiled=True)  82.7 us
    unnamed x1, blocking collectives  78.9 us
    psum x1, blocking collectives, on_device(): electron = lax.psum(elec_local, 'pb')  69.8 us
    dot_general x1, matrix products, block_terms(): jnp.einsum('imc,binc->bmnc', eig_kq, right, preferred_element_type=jnp.fl...  69.3 us
    reshape x1, local copies, waits for them, and re-layouts, block_terms(): bloch = bloch.reshape(n_modes, n_bands, n_bands, columns)  47.2 us
    dot_general x1, matrix products, block_terms(): jnp.einsum('bmjc,jnc->bmnc', modal, eig_k_cols, preferred_element_type=jn...  23 us
  transfers between devices with their start and end apart: 2, of which 0 were waited for; matrix products, arithmetic and copies ran while one was open for 3% of the time, Pallas kernels for 0%

commit v1 on v0

--- a/solution.py
+++ b/solution.py
@@ -6,6 +6,12 @@
 
 SIGMA = 0.1
 THERMAL_ENERGY_KT = 0.2
+
+
+def gather_and_add(block, mesh_axis):
+    parts = lax.all_gather(block, mesh_axis, axis=0, tiled=False)
+    result = parts.sum(axis=0)
+    return result
 
 
 def phase_table(lattice, kpoint_rows):
@@ -101,7 +107,7 @@
     elec_local = elec_cols[0].T * (1.0 / (total_q * n_modes * n_bands))
     phon_local = phon.T * (1.0 / (total_k * n_bands))
     phonon = lax.psum(phon_local, ("ka", "row"))
-    electron = lax.psum(elec_local, "pb")
+    electron = gather_and_add(elec_local, "pb")
     return (electron, phonon)
 
 

time: 555 us -> 525 us (0.946)
  blocking collectives: 372 us -> 343 us
    psum x1 -> x0, blocking collectives: 69.8 us -> none  [on_device(): electron = lax.psum(elec_local, 'pb')]
    all_gather x0 -> x1, blocking collectives: none -> 42.2 us  [gather_and_add(): parts = lax.all_gather(block, mesh_axis, axis=0, tiled=False)]
where the time goes in v1:
time: 525 us
  blocking collectives  343 us (65%)
  matrix products  100 us (19%)
  local copies, waits for them, and re-layouts  62.4 us (12%)
  between operations  14.9 us (3%)
    psum x1, blocking collectives, on_device(): phonon = lax.psum(phon_local, ('ka', 'row'))  139 us
    all_gather x1, blocking collectives, on_device(): lax.all_gather(energies, ('ka', 'row'), axis=0, tiled=True)  82.7 us
    unnamed x1, blocking collectives  78.9 us
    dot_general x1, matrix products, block_terms(): jnp.einsum('imc,binc->bmnc', eig_kq, right, preferred_element_type=jnp.fl...  69.3 us
    reshape x1, local copies, waits for them, and re-layouts, block_terms(): bloch = bloch.reshape(n_modes, n_bands, n_bands, columns)  47.2 us
    all_gather x1, blocking collectives, gather_and_add(): parts = lax.all_gather(block, mesh_axis, axis=0, tiled=False)  42.2 us
    dot_general x1, matrix products, block_terms(): jnp.einsum('bmjc,jnc->bmnc', modal, eig_k_cols, preferred_element_type=jn...  23 us
  transfers between devices with their start and end apart: 2, of which 0 were waited for; matrix products, arithmetic and copies ran while one was open for 3% of the time, Pallas kernels for 0%

profile of v1, /device:TPU:40, one launch (start us, length us, event | category | flops | bytes accessed | tf_op | source)
XLA Modules:
  0.0 524.8 jit_solution(6063365332447195264)
XLA Ops:
  7.2 1.7 copy.47
  9.0 1.8 copy.49
  11.2 0.7 convert_element_type.50
  11.8 1.3 dynamic-slice.8
  13.8 0.8 convert_dynamic-update-slice_fusion
  14.5 78.9 %all-reduce = f32[1024]{0:T(1024)S(1)} all-reduce(f32[1024]{0:T(1024)S(1)} %convert_dynamic-update-slice_fusion), channel_id=1, replica_groups=mesh['ka'=8,'pb'=16,'row'=4] {'ka','row'}, use_global_device_ids=true, to_apply=%add | all-reduce | flops 1024 | bytes 8192
  93.6 1.0 gather_fusion.2
  94.6 0.8 copy.79
  95.5 0.1 copy.62
  95.7 82.7 %all-gather.1 = f32[32,32,24]{1,2,0:T(8,128)S(1)} all-gather(f32[1,32,24]{1,2,0:T(8,128)} %bitcast.95), channel_id=1, replica_groups=mesh['ka'=8,'pb'=16,'row'=4] {'ka','row'}, dimensions={0}, use_global_device_ids=true | all-gather | bytes 101376 | tf_op jit(solution)/shard_map/all_gather | solution.py:81
  178.4 0.2 copy.57
  178.8 0.1 copy.61
  178.9 0.1 copy.65
  179.0 0.7 gather_fusion.1
  179.8 0.1 copy.66
  179.9 0.1 copy.59
  180.0 0.8 constant_dynamic-slice_fusion.1
  180.8 2.2 broadcast_subtract_fusion
  182.9 0.9 dynamic-slice_bitcast_fusion
  183.9 0.1 copy.48
  184.0 3.5 gather_fusion
  187.6 8.0 %fusion.4 = bf16[20736,4,32]{0,2,1:T(8,128)(2,1)} fusion(bf16[4,64,20736]{2,0,1:T(4,128)(2,1)} %all-gather.8.cloned.1.call-done, f32[32]{0:T(128)S(1)} %get-tuple-element.18, f32[64]{0:T(128)S(1)} %get-tuple-element.15, f32[32]{0:T(128)S(1)} %get-tuple-element.19, f32[64]{0:T(128)S(1)} %get-tuple-element.16, f32[32]{0:T(128)S(1)} %get-tuple-element.17, ...), kind=kOutput, calls=%fused_computation.10 | convolution fusion | flops 342407168 | bytes 15926400 | tf_op jit(solution)/shard_map/qrf,rk->fqk/dot_general | solution.py:36
  195.6 47.2 %reshape.257 = bf16[36,24,24,128]{2,1,0,3:T(8,128)(2,1)} reshape(bf16[20736,4,32]{0,2,1:T(8,128)(2,1)} %fusion.4) | data formatting | bytes 10616832 | tf_op jit(solution)/shard_map/reshape | solution.py:39
  242.8 0.1 tile.10
  242.9 0.2 broadcast_in_dim.40.clone
  243.1 23.0 %convert_bitcast_fusion = bf16[36,24,24,128]{0,2,1,3:T(8,128)(2,1)} fusion(bf16[24,24,128,1]{0,1,3,2:T(8,128)(2,1)S(1)} %bitcast.88, bf16[36,36,128,1]{1,0,3,2:T(8,128)(2,1)S(1)} %bitcast.87, bf16[36,24,24,128]{2,1,0,3:T(8,128)(2,1)} %reshape.257), kind=kOutput, calls=%fused_computation.15 | convolution fusion | flops 323813376 | bytes 11096064 | tf_op jit(solution)/shard_map/bmjc,jnc->bmnc/dot_general | solution.py:45
  266.1 69.3 %multiply_reduce_fusion = (f32[36,128]{0,1:T(8,128)S(1)}, f32[24,128]{0,1:T(8,128)S(1)}) fusion(f32[24,24,128]{0,1,2:T(8,128)} %get-tuple-element.22, f32[24,128]{0,1:T(8,128)S(1)} %copy.63, f32[24,128]{0,1:T(8,128)S(1)} %copy.62, f32[36,128]{0,1:T(8,128)S(1)} %bitcast.92, f32[24,24,128]{0,1,2:T(8,128)} %get-tuple-element.23, ...), kind=kOutput, calls=%fused_computation.6 | convolution fusion | flops 159318528 | bytes 6119552 | tf_op jit(solution)/shard_map/imc,binc->bmnc/dot_general | solution.py:48
  335.5 0.1 copy.78
  335.6 138.9 %psum.7 = f32[4,36]{0,1:T(8,128)S(1)} all-reduce(f32[4,36]{0,1:T(8,128)S(1)} %multiply_bitcast_fusion), channel_id=1, replica_groups=mesh['ka'=8,'pb'=16,'row'=4] {'ka','row'}, use_global_device_ids=true, to_apply=%region_5.6 | all-reduce | flops 144 | bytes 1152 | tf_op jit(solution)/shard_map/psum | solution.py:109
  474.5 0.7 copy.68
  475.2 42.2 %all-gather.2 = f32[16,32,24]{1,2,0:T(8,128)S(1)} all-gather(f32[1,32,24]{1,2,0:T(8,128)S(1)} %copy.64), channel_id=2, replica_groups=mesh['ka'=8,'pb'=16,'row'=4] {'pb'}, dimensions={0}, use_global_device_ids=true | all-gather | bytes 52224 | tf_op jit(solution)/shard_map/all_gather | solution.py:12
  517.4 0.6 reduce_sum.47
  (40 shorter events, 1.2 us)
Async XLA Ops:
  7.2 3.7 copy-start
  7.2 175.7 %all-gather.6.cloned.1.call-start = ((), (), s32[]{:S(2)}) async-start(), calls=%async_computation | async-start | bytes 6488064 | tf_op jit(solution)/shard_map/all_gather | solution.py:79
  9.0 178.6 %all-gather.8.cloned.1.call-start = ((), (), s32[]{:S(2)}) async-start(), calls=%async_computation.1 | async-start | bytes 10948608 | tf_op jit(solution)/shard_map/all_gather | solution.py:88
  243.1 23.0 %copy-start.2 = (f32[4,36]{1,0:T(4,128)S(1)}, f32[4,36]{1,0:T(4,128)}, u32[]{:S(2)}) copy-start(f32[4,36]{1,0:T(4,128)} %param.11) | copy-start | bytes 1732
  266.1 251.9 %copy-start.1 = (s32[4,1024]{1,0:T(4,128)S(1)}, s32[4,1024]{1,0:T(4,128)}, u32[]{:S(2)}) copy-start(s32[4,1024]{1,0:T(4,128)} %param.15) | copy-start | bytes 49156
Sparse Core Ops, SparseCore 0:
  11.1 75.5 all-gather.5
  89.9 93.6 all-gather.7

commit v2 on v0

--- a/solution.py
+++ b/solution.py
@@ -100,7 +100,9 @@
     elec_cols[0] = elec
     elec_local = elec_cols[0].T * (1.0 / (total_q * n_modes * n_bands))
     phon_local = phon.T * (1.0 / (total_k * n_bands))
-    phonon = lax.psum(phon_local, ("ka", "row"))
+    phonon = phon_local
+    for k0 in ("row", "ka"):
+        phonon = lax.psum(phonon, k0)
     electron = lax.psum(elec_local, "pb")
     return (electron, phonon)
 

time: 555 us -> 458 us (0.83)
  blocking collectives: 372 us -> 275 us
    psum x1 -> x2, blocking collectives: 140 us -> 43.7 us  [on_device(): phonon = lax.psum(phonon, k0)]
  transfers between devices with their start and end apart: 2 -> 2, of which waited for: 0 -> 0; matrix products, arithmetic and copies ran while one was open for 3% -> 4% of each run, Pallas kernels for 0% -> 0%
where the time goes in v2:
time: 458 us; the launch traced here: 457 us
  blocking collectives  275 us (60%)
  matrix products  100 us (22%)
  local copies, waits for them, and re-layouts  63 us (14%)
  between operations  14.9 us (3%)
    all_gather x1, blocking collectives, on_device(): lax.all_gather(energies, ('ka', 'row'), axis=0, tiled=True)  82.7 us
    unnamed x1, blocking collectives  78.9 us
    psum x1, blocking collectives, on_device(): electron = lax.psum(elec_local, 'pb')  69.8 us
    dot_general x1, matrix products, block_terms(): jnp.einsum('imc,binc->bmnc', eig_kq, right, preferred_element_type=jnp.fl...  69.3 us
    reshape x1, local copies, waits for them, and re-layouts, block_terms(): bloch = bloch.reshape(n_modes, n_bands, n_bands, columns)  47.2 us
    psum x2, blocking collectives, on_device(): phonon = lax.psum(phonon, k0)  43.7 us
    dot_general x1, matrix products, block_terms(): jnp.einsum('bmjc,jnc->bmnc', modal, eig_k_cols, preferred_element_type=jn...  23 us
  transfers between devices with their start and end apart: 2, of which 0 were waited for; matrix products, arithmetic and copies ran while one was open for 4% of the time, Pallas kernels for 0%

profile of v2, /device:TPU:40, one launch (start us, length us, event | category | flops | bytes accessed | tf_op | source)
XLA Modules:
  0.0 457.2 jit_solution(1038445209698914054)
XLA Ops:
  7.2 1.7 copy.47
  9.0 1.8 copy.49
  11.2 0.7 convert_element_type.50
  11.8 1.3 dynamic-slice.8
  13.8 0.8 convert_dynamic-update-slice_fusion
  14.5 78.9 %all-reduce = f32[1024]{0:T(1024)S(1)} all-reduce(f32[1024]{0:T(1024)S(1)} %convert_dynamic-update-slice_fusion), channel_id=1, replica_groups=mesh['ka'=8,'pb'=16,'row'=4] {'ka','row'}, use_global_device_ids=true, to_apply=%add | all-reduce | flops 1024 | bytes 8192
  93.6 1.0 gather_fusion.2
  94.6 0.8 copy.79
  95.5 0.1 copy.62
  95.7 82.7 %all-gather = f32[32,32,24]{1,2,0:T(8,128)S(1)} all-gather(f32[1,32,24]{1,2,0:T(8,128)} %bitcast.93), channel_id=1, replica_groups=mesh['ka'=8,'pb'=16,'row'=4] {'ka','row'}, dimensions={0}, use_global_device_ids=true | all-gather | bytes 101376 | tf_op jit(solution)/shard_map/all_gather | solution.py:75
  178.4 0.2 copy.57
  178.8 0.1 copy.61
  178.9 0.1 copy.64
  179.0 0.7 gather_fusion.1
  179.8 0.1 copy.65
  180.0 0.8 constant_dynamic-slice_fusion.1
  180.8 2.2 broadcast_subtract_fusion
  182.9 0.9 dynamic-slice_bitcast_fusion
  183.9 0.1 copy.48
  184.0 3.5 gather_fusion
  187.6 8.0 %fusion.4 = bf16[20736,4,32]{0,2,1:T(8,128)(2,1)} fusion(bf16[4,64,20736]{2,0,1:T(4,128)(2,1)} %all-gather.6.cloned.1.call-done, f32[32]{0:T(128)S(1)} %get-tuple-element.18, f32[64]{0:T(128)S(1)} %get-tuple-element.15, f32[32]{0:T(128)S(1)} %get-tuple-element.19, f32[64]{0:T(128)S(1)} %get-tuple-element.16, f32[32]{0:T(128)S(1)} %get-tuple-element.17, ...), kind=kOutput, calls=%fused_computation.10 | convolution fusion | flops 342407168 | bytes 15926400 | tf_op jit(solution)/shard_map/qrf,rk->fqk/dot_general | solution.py:30
  195.6 47.2 %reshape.253 = bf16[36,24,24,128]{2,1,0,3:T(8,128)(2,1)} reshape(bf16[20736,4,32]{0,2,1:T(8,128)(2,1)} %fusion.4) | data formatting | bytes 10616832 | tf_op jit(solution)/shard_map/reshape | solution.py:33
  242.8 0.1 tile.10
  242.9 0.2 broadcast_in_dim.40.clone
  243.1 23.0 %convert_bitcast_fusion = bf16[36,24,24,128]{0,2,1,3:T(8,128)(2,1)} fusion(bf16[24,24,128,1]{0,1,3,2:T(8,128)(2,1)S(1)} %bitcast.86, bf16[36,36,128,1]{1,0,3,2:T(8,128)(2,1)S(1)} %bitcast.85, bf16[36,24,24,128]{2,1,0,3:T(8,128)(2,1)} %reshape.253), kind=kOutput, calls=%fused_computation.15 | convolution fusion | flops 323813376 | bytes 11096064 | tf_op jit(solution)/shard_map/bmjc,jnc->bmnc/dot_general | solution.py:39
  266.1 69.3 %multiply_reduce_fusion = (f32[36,128]{0,1:T(8,128)S(1)}, f32[24,128]{0,1:T(8,128)S(1)}) fusion(f32[24,24,128]{0,1,2:T(8,128)} %get-tuple-element.22, f32[24,128]{0,1:T(8,128)S(1)} %copy.63, f32[24,128]{0,1:T(8,128)S(1)} %copy.62, f32[36,128]{0,1:T(8,128)S(1)} %bitcast.90, f32[24,24,128]{0,1,2:T(8,128)} %get-tuple-element.23, ...), kind=kOutput, calls=%fused_computation.6 | convolution fusion | flops 159318528 | bytes 6119552 | tf_op jit(solution)/shard_map/imc,binc->bmnc/dot_general | solution.py:42
  335.5 69.8 %psum.21 = f32[32,24]{1,0:T(8,128)S(1)} all-reduce(f32[32,24]{1,0:T(8,128)S(1)} %multiply_bitcast_fusion.1), channel_id=1, replica_groups=mesh['ka'=8,'pb'=16,'row'=4] {'pb'}, use_global_device_ids=true, to_apply=%region_2.3 | all-reduce | flops 768 | bytes 6144 | tf_op jit(solution)/shard_map/psum | solution.py:106
  405.3 0.7 copy.67
  405.9 0.1 copy.78
  406.0 16.5 %psum.22 = f32[4,36]{0,1:T(8,128)S(1)} all-reduce(f32[4,36]{0,1:T(8,128)S(1)} %multiply_bitcast_fusion), channel_id=1, replica_groups=mesh['ka'=8,'pb'=16,'row'=4] {'row'}, use_global_device_ids=true, to_apply=%region_5.6 | all-reduce | flops 144 | bytes 1152 | tf_op jit(solution)/shard_map/psum | solution.py:105
  422.5 27.2 %psum.23 = f32[4,36]{0,1:T(8,128)S(1)} all-reduce(f32[4,36]{0,1:T(8,128)S(1)} %psum.22), channel_id=1, replica_groups=mesh['ka'=8,'pb'=16,'row'=4] {'ka'}, use_global_device_ids=true, to_apply=%region_6.7 | all-reduce | flops 144 | bytes 1152 | tf_op jit(solution)/shard_map/psum | solution.py:105
  449.7 0.7 copy.68
  (40 shorter events, 1.2 us)
Async XLA Ops:
  7.2 3.7 copy-start
  7.2 175.7 %all-gather.4.cloned.1.call-start = ((), (), s32[]{:S(2)}) async-start(), calls=%async_computation | async-start | bytes 6488064 | tf_op jit(solution)/shard_map/all_gather | solution.py:73
  9.0 178.6 %all-gather.6.cloned.1.call-start = ((), (), s32[]{:S(2)}) async-start(), calls=%async_computation.1 | async-start | bytes 10948608 | tf_op jit(solution)/shard_map/all_gather | solution.py:82
  243.1 23.0 %copy-start.2 = (f32[4,36]{1,0:T(4,128)S(1)}, f32[4,36]{1,0:T(4,128)}, u32[]{:S(2)}) copy-start(f32[4,36]{1,0:T(4,128)} %param.11) | copy-start | bytes 1732
  266.1 184.3 %copy-start.1 = (s32[4,1024]{1,0:T(4,128)S(1)}, s32[4,1024]{1,0:T(4,128)}, u32[]{:S(2)}) copy-start(s32[4,1024]{1,0:T(4,128)} %param.15) | copy-start | bytes 49156
Sparse Core Ops, SparseCore 0:
  11.1 75.5 all-gather.3
  89.9 93.6 all-gather.5
